TPU v7x, 256 devices: a whole 4x4x8 slice. The times are simulated.
256 devices in a mesh: lat: 16 (over x, y_hi, core), lon: 16 (over y_lo, z).
Axes of the slice: x: 4, y: 4 (y_hi: 2, y_lo: 2; y = y_hi * 2 + y_lo), z: 8, core: 2. Of those that a mesh axis runs over, the one named last changes fastest.
Arguments:
- feature: bfloat16 [512, 512, 384], P('lat', 'lon'), may hold values from -6 to 6
- coverage: int32 [512, 512], P('lat', 'lon'), may hold values 0 or 1
- band_rows: int32 [16], replicated, may hold values from 3 to 32, as said below
- depth_weight: bfloat16 [7, 7, 384], replicated, may hold values from -0.875 to 0.875
- norm_gain: float32 [384], replicated, may hold values from 0.25 to 1.75
- norm_shift: float32 [384], replicated, may hold values from -3 to 3
- up_weight: bfloat16 [384, 1536], P('lon'), may hold values from -0.3125 to 0.3125
- up_bias: float32 [1536], replicated, may hold values from -3 to 3
- down_weight: bfloat16 [1536, 384], P('lon'), may hold values from -0.15625 to 0.15625
- down_bias: float32 [384], replicated, may hold values from -3 to 3
- layer_scale: float32 [384], replicated, may hold values from 0.3 to 1.5
- cotangent: bfloat16 [512, 512, 384], P('lat', 'lon'), may hold values from -6 to 6
Outputs:
- block_out: bfloat16 [512, 512, 384], P('lat', 'lon')
- grad_in: bfloat16 [512, 512, 384], P('lat', 'lon')
- grad_up: float32 [384, 1536], P('lon')
- grad_down: float32 [1536, 384], P('lon')
- grad_depth: float32 [7, 7, 384], replicated
Inputs may be any that keep to these rules, and one draw needn't show every extreme that they name: `band_rows`: every band has 3 or more rows, the bands' rows sum to 256, and one band has exactly 32.
All inputs are finite; a program needn't handle non-finite values. No bound on the sum of `coverage` on one device may be relied on, other than what follows from the above.
Results may differ from a plain program's by a relative error of at most 0.0066.
Values may be sent and summed in bfloat16 or wider, within the bound.
A program may use at most 64 MiB of HBM per device.

v0:
```python
import math
import jax
import jax.numpy as jnp
from jax import lax
from jax.sharding import PartitionSpec as P

BAND_MEAN = 16
SQRT_TWO_PI = 0.7978845608028654
CUBIC = 0.044715
EPSILON = 1e-06


def padded(array, sides, width):
    for axis, dim in sides:
        size, length = (lax.axis_size(axis), array.shape[dim])
        up = [(i, (i + 1) % size) for i in range(size)]
        down = [(j, i) for i, j in up]
        last = lax.slice_in_dim(array, length - width, length, axis=dim)
        initial = lax.slice_in_dim(array, 0, width, axis=dim)
        before = lax.ppermute(last, axis, up)
        after = lax.ppermute(initial, axis, down)
        array = jnp.concatenate([before, array, after], axis=dim)
    return array


def shifted(block, axis, distance):
    devices = range(lax.axis_size(axis))
    route = [(i - distance, i) for i in devices if i - distance in devices]
    return lax.ppermute(block, axis, route)


def smooth_gate(pre_act):
    argument = SQRT_TWO_PI * (pre_act + CUBIC * pre_act * pre_act * pre_act)
    return 0.5 * pre_act * (1.0 + jnp.tanh(argument))


def smooth_slope(pre_act):
    argument = SQRT_TWO_PI * (pre_act + CUBIC * pre_act * pre_act * pre_act)
    tangent = jnp.tanh(argument)
    return 0.5 * (1.0 + tangent) + 0.5 * pre_act * (1.0 - tangent * tangent) * SQRT_TWO_PI * (
        1.0 + 3.0 * CUBIC * pre_act * pre_act
    )


def extend(field, live_rows):
    widened = padded(field, (("lon", 1),), 3)
    last_rows = lax.dynamic_slice_in_dim(widened, live_rows - 3, 3, 0)
    from_above = shifted(last_rows, "lat", 1)
    from_below = shifted(widened[:3], "lat", -1)
    zero_rows = jnp.zeros((3,) + widened.shape[1:], widened.dtype)
    stacked = jnp.concatenate([from_above, widened, zero_rows], axis=0)
    return lax.dynamic_update_slice_in_dim(stacked, from_below, live_rows + 3, 0)


def shards(
    feature,
    coverage,
    band_rows,
    depth_weight,
    norm_gain,
    norm_shift,
    up_weight,
    up_bias,
    down_weight,
    down_bias,
    layer_scale,
    cotangent,
):
    rows_max, tile_cols, channels = feature.shape
    kernel = depth_weight.shape[0]
    live_rows = lax.dynamic_index_in_dim(band_rows, lax.axis_index("lat"), 0, keepdims=False)
    inside = jnp.arange(rows_max, dtype=jnp.int32) < live_rows
    covered = jnp.where(inside[:, None], coverage, 0).astype(jnp.bfloat16)
    masked = feature * covered[:, :, None]
    framed = extend(masked, live_rows)
    depth_out = jnp.zeros((rows_max, tile_cols, channels), jnp.float32)
    for row_off in range(kernel):
        for col_off in range(kernel):
            depth_out = depth_out + framed[
                row_off : row_off + rows_max, col_off : col_off + tile_cols
            ].astype(jnp.float32) * depth_weight[row_off, col_off].astype(jnp.float32)
    full_up, full_down = (
        lax.all_gather(up_weight, "lon", axis=0, tiled=True),
        lax.all_gather(down_weight, "lon", axis=0, tiled=True),
    )
    depth_rows = depth_out.reshape(-1, channels)
    center = jnp.mean(depth_rows, axis=-1, keepdims=True)
    offset = depth_rows - center
    scale_inv = lax.rsqrt(jnp.mean(offset * offset, axis=-1, keepdims=True) + EPSILON)
    standard = offset * scale_inv
    normed = (standard * norm_gain + norm_shift).astype(jnp.bfloat16)
    before = jnp.dot(normed, full_up, preferred_element_type=jnp.float32) + up_bias
    active = smooth_gate(before).astype(jnp.bfloat16)
    branch = jnp.dot(active, full_down, preferred_element_type=jnp.float32) + down_bias
    result = (feature.reshape(-1, channels).astype(jnp.float32) + layer_scale * branch).astype(
        jnp.bfloat16
    )
    cot_live = jnp.where(inside[:, None, None], cotangent, jnp.zeros_like(cotangent)).reshape(
        -1, channels
    )
    upstream = (layer_scale * cot_live.astype(jnp.float32)).astype(jnp.bfloat16)
    sum_down = lax.dot_general(
        active, upstream, (((0,), (0,)), ((), ())), preferred_element_type=jnp.float32
    )
    back_active = lax.dot_general(
        upstream, full_down, (((1,), (1,)), ((), ())), preferred_element_type=jnp.float32
    )
    back_before = (back_active * smooth_slope(before)).astype(jnp.bfloat16)
    sum_up = lax.dot_general(
        normed, back_before, (((0,), (0,)), ((), ())), preferred_element_type=jnp.float32
    )
    back_normed = lax.dot_general(
        back_before, full_up, (((1,), (1,)), ((), ())), preferred_element_type=jnp.float32
    )
    back_unit = back_normed * norm_gain
    back_depth = scale_inv * (
        back_unit
        - jnp.mean(back_unit, axis=-1, keepdims=True)
        - standard * jnp.mean(back_unit * standard, axis=-1, keepdims=True)
    )
    back_depth = back_depth.astype(jnp.bfloat16).reshape(rows_max, tile_cols, channels)
    framed_back = extend(back_depth, live_rows)
    spread = jnp.zeros((rows_max, tile_cols, channels), jnp.float32)
    tap_list = []
    for row_off in range(kernel):
        for col_off in range(kernel):
            spread = spread + framed_back[
                6 - row_off : 6 - row_off + rows_max, 6 - col_off : 6 - col_off + tile_cols
            ].astype(jnp.float32) * depth_weight[row_off, col_off].astype(jnp.float32)
            tap_list.append(
                jnp.sum(
                    framed[row_off : row_off + rows_max, col_off : col_off + tile_cols].astype(
                        jnp.float32
                    )
                    * back_depth.astype(jnp.float32),
                    axis=(0, 1),
                )
            )
    grad_local = (
        cotangent.astype(jnp.float32) + covered.astype(jnp.float32)[:, :, None] * spread
    ).astype(jnp.bfloat16)
    grad_in = jnp.where(inside[:, None, None], grad_local, jnp.zeros_like(grad_local))
    block_out = jnp.where(
        inside[:, None, None],
        result.reshape(rows_max, tile_cols, channels),
        jnp.zeros_like(feature),
    )
    rscale = 1.0 / math.sqrt(BAND_MEAN * lax.axis_size("lat") * tile_cols * lax.axis_size("lon"))
    tap_terms = jnp.stack(tap_list, axis=0).reshape(kernel, kernel, channels)
    grad_depth = lax.psum(tap_terms, ("lat", "lon")) * rscale
    up_part, down_part = (
        lax.psum_scatter(sum_up, "lon", scatter_dimension=0, tiled=True),
        lax.psum_scatter(sum_down, "lon", scatter_dimension=0, tiled=True),
    )
    up_part, down_part = lax.psum((up_part, down_part), "lat")
    return (block_out, grad_in, up_part * rscale, down_part * rscale, grad_depth)


def solution(mesh):
    placed = (
        P("lat", "lon", None),
        P("lat", "lon"),
        P(),
        P(),
        P(),
        P(),
        P("lon", None),
        P(),
        P("lon", None),
        P(),
        P(),
        P("lat", "lon", None),
    )
    return jax.shard_map(
        shards,
        mesh=mesh,
        in_specs=placed,
        out_specs=(
            P("lat", "lon", None),
            P("lat", "lon", None),
            P("lon", None),
            P("lon", None),
            P(),
        ),
        check_vma=False,
    )
```

profile of v0, /device:TPU:8, one launch (start us, length us, event | category | flops | bytes accessed | tf_op | source)
XLA Modules:
  0.0 711.5 jit_solution(1951065629706237876)
XLA Ops:
  8.0 1.2 dynamic_slice.10
  10.7 1.3 broadcast_multiply_fusion
  12.1 2.0 collective-permute-start
  14.1 3.9 collective-permute-start.1
  22.6 1.5 collective-permute-start.2
  24.7 1.3 collective-permute-start.3
  27.1 3.4 collective-permute-done.3
  30.9 12.5 %fusion.109 = (f32[32,32]{1,0:T(8,128)S(1)}, f32[32,32,384]{2,1,0:T(8,128)S(1)}) fusion(f32[384]{0:T(512)} %get-tuple-element.103, bf16[38,38,384]{2,1,0:T(8,128)(2,1)S(1)} %constant_dynamic-update-slice_fusion.1, f32[384]{0:T(512)} %get-tuple-element.104, f32[384]{0:T(512)S(1)} %get-tuple-element.57, f32[384]{0:T(512)S(1)} %get-tuple-element.58, ...), kind=kLoop, calls=%fused_computation.289 | loop fusion | flops 57801728 | bytes 40187392 | tf_op jit(solution)/shard_map/reduce_sum | solution.py:87
  44.2 1.2 add_convert_fusion.1
  45.4 36.1 %all-gather.3.cloned.1.call-done = bf16[384,1536]{1,0:T(8,128)(2,1)} async-done(((bf16[24,1536]{1,0:T(8,128)(2,1)}), bf16[384,1536]{1,0:T(8,128)(2,1)}) %all-gather.3.cloned.1.call-update) | async-done | bytes 1179664 | tf_op jit(solution)/shard_map/all_gather | solution.py:83
  81.5 7.8 %multiply_convert_fusion = (bf16[1024,1536]{1,0:T(8,128)(2,1)}, f32[1024,1536]{1,0:T(8,128)}) fusion(f32[1536]{0:T(1024)} %param.19, bf16[1024,384]{1,0:T(8,128)(2,1)} %add_convert_fusion.1, bf16[384,1536]{1,0:T(8,128)(2,1)} %all-gather.3.cloned.1.call-done), kind=kOutput, calls=%fused_computation.58 | convolution fusion | flops 1223688192 | bytes 11409408 | tf_op jit(solution)/shard_map/dot_general | solution.py:92
  89.3 61.2 %all-gather.5.cloned.1.call-done = bf16[1536,384]{1,0:T(8,128)(2,1)} async-done(((bf16[96,384]{1,0:T(8,128)(2,1)}), bf16[1536,384]{1,0:T(8,128)(2,1)}) %all-gather.5.cloned.1.call-update) | async-done | bytes 1179664 | tf_op jit(solution)/shard_map/all_gather | solution.py:84
  150.5 4.2 fusion.105
  157.3 5.4 fusion.6
  162.7 2.0 fusion.107
  164.8 5.0 fusion.103
  169.7 3.0 fusion.67
  172.8 4.0 fusion.85
  178.2 5.2 fusion.116
  184.6 4.7 fusion.115
  190.1 3.5 collective-permute-start.5
  193.6 2.6 collective-permute-done.4
  197.2 1.3 collective-permute-start.6
  198.5 218.1 %all-reduce.4.cloned.1.call-done = f32[7,7,384]{2,1,0:T(8,128)} async-done(((f32[7,7,384]{2,1,0:T(8,128)}), f32[7,7,384]{2,1,0:T(8,128)}) %all-reduce.4.cloned.1.call-update) | async-done | bytes 75280 | tf_op jit(solution)/shard_map/psum | solution.py:150
  416.6 1.5 broadcast_multiply_fusion.3
  418.1 1.3 collective-permute-start.7
  421.3 68.6 %reduce-scatter.5.cloned.1.call-done = f32[96,384]{1,0:T(8,128)} async-done(((f32[1536,384]{1,0:T(8,128)}), f32[96,384]{1,0:T(8,128)}) %reduce-scatter.5.cloned.1.call-update) | async-done | bytes 147472 | tf_op jit(solution)/shard_map/reduce_scatter | solution.py:153
  489.9 73.4 %reduce-scatter.3.cloned.1.call-done = f32[24,1536]{1,0:T(8,128)} async-done(((f32[384,1536]{1,0:T(8,128)}), f32[24,1536]{1,0:T(8,128)}) %reduce-scatter.3.cloned.1.call-update) | async-done | bytes 147472 | tf_op jit(solution)/shard_map/reduce_scatter | solution.py:152
  563.8 12.6 %broadcast_select_fusion = bf16[32,32,384]{2,1,0:T(8,128)(2,1)} fusion(pred[32]{0:T(512)(128)(4,1)} %copy-done.85, f32[384]{0:T(512)} %get-tuple-element.103, bf16[38,38,384]{2,1,0:T(8,128)(2,1)S(1)} %constant_dynamic-update-slice_fusion, f32[384]{0:T(512)} %get-tuple-element.104, f32[384]{0:T(512)S(1)} %copy-done.46, f32[384]{0:T(512)S(1)} %copy-done.48, ...), kind=kLoop, calls=%fused_computation.221 | loop fusion | flops 59375616 | bytes 40187424 | tf_op jit(solution)/shard_map/jit(_where)/select_n | solution.py:142
  576.3 125.2 %all-reduce.6.cloned.1.call-done = (f32[24,1536]{1,0:T(8,128)}, f32[96,384]{1,0:T(8,128)}) async-done(((f32[24,1536]{1,0:T(8,128)}, f32[96,384]{1,0:T(8,128)}), (f32[24,1536]{1,0:T(8,128)}, f32[96,384]{1,0:T(8,128)})) %all-reduce.6.cloned.1.call-update) | async-done | bytes 294928 | tf_op jit(solution)/shard_map/psum | solution.py:155
  701.5 1.6 broadcast_multiply_fusion.2
  703.1 1.6 broadcast_multiply_fusion.1
  (287 shorter events, 14.7 us)
Async XLA Ops:
  7.2 74.3 %all-gather.3.cloned.1.call-start = ((), (), s32[]{:S(2)}) async-start(), calls=%async_computation.2 | async-start | bytes 1253376 | tf_op jit(solution)/shard_map/all_gather | solution.py:83
  7.9 142.6 %all-gather.5.cloned.1.call-start = ((), (), s32[]{:S(2)}) async-start(), calls=%async_computation.3 | async-start | bytes 1253376 | tf_op jit(solution)/shard_map/all_gather | solution.py:84
  12.1 9.8 %collective-permute-start = (bf16[32,3,384]{2,1,0:T(4,128)(2,1)S(1)}, bf16[32,3,384]{2,1,0:T(4,128)(2,1)S(1)}, u32[]{:S(2)}, u32[]{:S(2)}) collective-permute-start(bf16[32,3,384]{2,1,0:T(4,128)(2,1)S(1)} %get-tuple-element.118), channel_id=1, source_target_pairs={{0,1},{1,2},{2,3},{3,4},{4,5},{5,6},{6,7},{7,8},{8,9},{9,10},{10,1... | collective-permute-start | bytes 221192 | tf_op jit(solution)/shard_map/ppermute | solution.py:20
  14.1 7.9 %collective-permute-start.1 = (bf16[32,3,384]{2,1,0:T(4,128)(2,1)S(1)}, bf16[32,3,384]{2,1,0:T(4,128)(2,1)S(1)}, u32[]{:S(2)}, u32[]{:S(2)}) collective-permute-start(bf16[32,3,384]{2,1,0:T(4,128)(2,1)S(1)} %get-tuple-element.119), channel_id=1, source_target_pairs={{1,0},{2,1},{3,2},{4,3},{5,4},{6,5},{7,6},{8,7},{9,8},{10,9},{11,1... | collective-permute-start | bytes 221192 | tf_op jit(solution)/shard_map/ppermute | solution.py:21
  18.0 398.6 %all-reduce.4.cloned.1.call-start = ((), (), s32[]{:S(2)}) async-start(), calls=%async_computation.6 | async-start | bytes 172032 | tf_op jit(solution)/shard_map/psum | solution.py:150
  22.6 3.4 collective-permute-start.2
  24.7 5.8 collective-permute-start.3
  178.2 311.8 %reduce-scatter.5.cloned.1.call-start = ((), (), s32[]{:S(2)}) async-start(), calls=%async_computation.5 | async-start | bytes 2506752 | tf_op jit(solution)/shard_map/reduce_scatter | solution.py:153
  183.4 379.9 %reduce-scatter.3.cloned.1.call-start = ((), (), s32[]{:S(2)}) async-start(), calls=%async_computation.4 | async-start | bytes 2506752 | tf_op jit(solution)/shard_map/reduce_scatter | solution.py:152
  189.3 512.2 %all-reduce.6.cloned.1.call-start = ((), (), s32[]{:S(2)}) async-start(), calls=%async_computation.7 | async-start | bytes 589824 | tf_op jit(solution)/shard_map/psum | solution.py:155
  189.4 6.8 collective-permute-start.4
  190.1 6.1 collective-permute-start.5
  196.8 366.5 %copy-start.1 = (bf16[32,32,384]{2,1,0:T(8,128)(2,1)S(1)}, bf16[32,32,384]{2,1,0:T(8,128)(2,1)}, u32[]{:S(2)}) copy-start(bf16[32,32,384]{2,1,0:T(8,128)(2,1)} %param.23) | copy-start | bytes 2359300
  196.8 366.5 %copy-start.8 = (f32[384]{0:T(512)S(1)}, f32[384]{0:T(512)}, u32[]{:S(2)}) copy-start(f32[384]{0:T(512)} %copy-done.7) | copy-start | bytes 4612
  196.8 366.5 %copy-start.10 = (f32[384]{0:T(512)S(1)}, f32[384]{0:T(512)}, u32[]{:S(2)}) copy-start(f32[384]{0:T(512)} %copy-done.9) | copy-start | bytes 4612
  196.8 366.5 %copy-start.12 = (f32[384]{0:T(512)S(1)}, f32[384]{0:T(512)}, u32[]{:S(2)}) copy-start(f32[384]{0:T(512)} %copy-done.11) | copy-start | bytes 4612
  196.9 366.5 %copy-start.14 = (f32[384]{0:T(512)S(1)}, f32[384]{0:T(512)}, u32[]{:S(2)}) copy-start(f32[384]{0:T(512)} %copy-done.13) | copy-start | bytes 4612
  196.9 366.5 %copy-start.16 = (f32[384]{0:T(512)S(1)}, f32[384]{0:T(512)}, u32[]{:S(2)}) copy-start(f32[384]{0:T(512)} %copy-done.15) | copy-start | bytes 4612
  196.9 366.5 %copy-start.18 = (f32[384]{0:T(512)S(1)}, f32[384]{0:T(512)}, u32[]{:S(2)}) copy-start(f32[384]{0:T(512)} %copy-done.17) | copy-start | bytes 4612
  196.9 366.5 %copy-start.20 = (f32[384]{0:T(512)S(1)}, f32[384]{0:T(512)}, u32[]{:S(2)}) copy-start(f32[384]{0:T(512)} %copy-done.19) | copy-start | bytes 4612
  196.9 366.5 %copy-start.22 = (f32[384]{0:T(512)S(1)}, f32[384]{0:T(512)}, u32[]{:S(2)}) copy-start(f32[384]{0:T(512)} %copy-done.21) | copy-start | bytes 4612
  196.9 366.5 %copy-start.24 = (f32[384]{0:T(512)S(1)}, f32[384]{0:T(512)}, u32[]{:S(2)}) copy-start(f32[384]{0:T(512)} %copy-done.23) | copy-start | bytes 4612
  196.9 366.5 %copy-start.26 = (f32[384]{0:T(512)S(1)}, f32[384]{0:T(512)}, u32[]{:S(2)}) copy-start(f32[384]{0:T(512)} %copy-done.25) | copy-start | bytes 4612
  196.9 366.5 %copy-start.28 = (f32[384]{0:T(512)S(1)}, f32[384]{0:T(512)}, u32[]{:S(2)}) copy-start(f32[384]{0:T(512)} %copy-done.27) | copy-start | bytes 4612
  196.9 366.5 %copy-start.30 = (f32[384]{0:T(512)S(1)}, f32[384]{0:T(512)}, u32[]{:S(2)}) copy-start(f32[384]{0:T(512)} %copy-done.29) | copy-start | bytes 4612
  196.9 366.5 %copy-start.32 = (f32[384]{0:T(512)S(1)}, f32[384]{0:T(512)}, u32[]{:S(2)}) copy-start(f32[384]{0:T(512)} %copy-done.31) | copy-start | bytes 4612
  197.0 366.5 %copy-start.34 = (f32[384]{0:T(512)S(1)}, f32[384]{0:T(512)}, u32[]{:S(2)}) copy-start(f32[384]{0:T(512)} %copy-done.33) | copy-start | bytes 4612
  197.0 366.5 %copy-start.36 = (f32[384]{0:T(512)S(1)}, f32[384]{0:T(512)}, u32[]{:S(2)}) copy-start(f32[384]{0:T(512)} %copy-done.35) | copy-start | bytes 4612
  197.0 366.5 %copy-start.38 = (f32[384]{0:T(512)S(1)}, f32[384]{0:T(512)}, u32[]{:S(2)}) copy-start(f32[384]{0:T(512)} %copy-done.37) | copy-start | bytes 4612
  197.0 366.5 %copy-start.40 = (f32[384]{0:T(512)S(1)}, f32[384]{0:T(512)}, u32[]{:S(2)}) copy-start(f32[384]{0:T(512)} %copy-done.39) | copy-start | bytes 4612
  197.2 222.2 %collective-permute-start.6 = (bf16[3,38,384]{2,1,0:T(8,128)(2,1)S(1)}, bf16[3,38,384]{2,1,0:T(8,128)(2,1)S(1)}, u32[]{:S(2)}, u32[]{:S(2)}) collective-permute-start(bf16[3,38,384]{2,1,0:T(8,128)(2,1)S(1)} %get-tuple-element.113), channel_id=1, source_target_pairs={{0,16},{16,32},{32,48},{48,64},{64,80},{80,96},{96,112},{112,128},... | collective-permute-start | bytes 262664 | tf_op jit(solution)/shard_map/ppermute | solution.py:29
  418.1 3.2 collective-permute-start.7
  (78 other events, 8612.5 us)
Sparse Core Ops, SparseCore 0:
  9.8 71.6 all-gather.2
  83.3 67.1 all-gather.4
  178.3 238.2 all-reduce.3
  419.0 70.8 reduce-scatter.4
  492.3 70.9 reduce-scatter.2
  565.9 135.5 all-reduce.5
where the time goes:
time: 712 us
  waiting for transfers between devices  590 us (83%)
  other arithmetic  51.7 us (7%)
  matrix products  29.3 us (4%)
  between operations  18.7 us (3%)
  starting transfers between devices  15.7 us (2%)
    psum x1, waiting for transfers between devices, shards(): grad_depth = lax.psum(tap_terms, ('lat', 'lon')) * rscale  218 us
    psum x1, waiting for transfers between devices, shards(): up_part, down_part = lax.psum((up_part, down_part), 'lat')  125 us
    reduce_scatter x1, waiting for transfers between devices, shards(): lax.psum_scatter(sum_up, 'lon', scatter_dimension=0, tiled=True)  73.4 us
    reduce_scatter x1, waiting for transfers between devices, shards(): lax.psum_scatter(sum_down, 'lon', scatter_dimension=0, tiled=True)  68.6 us
    all_gather x1, waiting for transfers between devices, shards(): lax.all_gather(down_weight, 'lon', axis=0, tiled=True)  61.2 us
    all_gather x1, waiting for transfers between devices, shards(): lax.all_gather(up_weight, 'lon', axis=0, tiled=True)  36.1 us
  transfers between devices with their start and end apart: 14, of which 9 were waited for; matrix products, arithmetic and copies ran while one was open for 8% of the time, Pallas kernels for 0%

commit v1 on v0

--- a/solution.py
+++ b/solution.py
@@ -147,7 +147,7 @@
     )
     rscale = 1.0 / math.sqrt(BAND_MEAN * lax.axis_size("lat") * tile_cols * lax.axis_size("lon"))
     tap_terms = jnp.stack(tap_list, axis=0).reshape(kernel, kernel, channels)
-    grad_depth = lax.psum(tap_terms, ("lat", "lon")) * rscale
+    grad_depth = lax.psum(lax.psum(tap_terms, "lon"), "lat") * rscale
     up_part, down_part = (
         lax.psum_scatter(sum_up, "lon", scatter_dimension=0, tiled=True),
         lax.psum_scatter(sum_down, "lon", scatter_dimension=0, tiled=True),

time: 712 us -> 611 us (0.86)
  waiting for transfers between devices: 590 us -> 487 us
    psum x1, waiting for transfers between devices: 218 us -> 99.9 us  [shards(): grad_depth = lax.psum(lax.psum(tap_terms, 'lon'), 'lat') * rscale]
    reduce_scatter x1, waiting for transfers between devices: 68.6 us -> 76.2 us  [shards(): lax.psum_scatter(sum_down, 'lon', scatter_dimension=0, tiled=True)]
  transfers between devices with their start and end apart: 14 -> 14, of which waited for: 9 -> 9; matrix products, arithmetic and copies ran while one was open for 8% -> 9% of each run, Pallas kernels for 0% -> 0%
where the time goes in v1:
time: 611 us; the launch traced here: 609 us
  waiting for transfers between devices  487 us (80%)
  other arithmetic  51.7 us (8%)
  matrix products  29.3 us (5%)
  between operations  18.7 us (3%)
  starting transfers between devices  15.7 us (3%)
    psum x1, waiting for transfers between devices, shards(): up_part, down_part = lax.psum((up_part, down_part), 'lat')  130 us
    psum x1, waiting for transfers between devices, shards(): grad_depth = lax.psum(lax.psum(tap_terms, 'lon'), 'lat') * rscale  99.9 us
    reduce_scatter x1, waiting for transfers between devices, shards(): lax.psum_scatter(sum_down, 'lon', scatter_dimension=0, tiled=True)  76.2 us
    reduce_scatter x1, waiting for transfers between devices, shards(): lax.psum_scatter(sum_up, 'lon', scatter_dimension=0, tiled=True)  73.6 us
    all_gather x1, waiting for transfers between devices, shards(): lax.all_gather(down_weight, 'lon', axis=0, tiled=True)  61.2 us
    all_gather x1, waiting for transfers between devices, shards(): lax.all_gather(up_weight, 'lon', axis=0, tiled=True)  36.1 us
    select_n x1, other arithmetic, shards(): jnp.where(inside[:, None, None], grad_local, jnp.zeros_like(grad_local))  12.6 us
    reduce_sum x1, other arithmetic, shards(): center = jnp.mean(depth_rows, axis=-1, keepdims=True)  12.5 us
  transfers between devices with their start and end apart: 14, of which 9 were waited for; matrix products, arithmetic and copies ran while one was open for 9% of the time, Pallas kernels for 0%

profile of v1, /device:TPU:8, one launch (start us, length us, event | category | flops | bytes accessed | tf_op | source)
XLA Modules:
  0.0 608.8 jit_solution(8314623124003333438)
XLA Ops:
  8.0 1.2 dynamic_slice.10
  10.7 1.3 broadcast_multiply_fusion
  12.1 2.0 collective-permute-start
  14.1 3.9 collective-permute-start.1
  22.6 1.5 collective-permute-start.2
  24.7 1.3 collective-permute-start.3
  27.1 3.4 collective-permute-done.3
  30.9 12.5 %fusion.109 = (f32[32,32]{1,0:T(8,128)S(1)}, f32[32,32,384]{2,1,0:T(8,128)S(1)}) fusion(f32[384]{0:T(512)} %get-tuple-element.103, bf16[38,38,384]{2,1,0:T(8,128)(2,1)S(1)} %constant_dynamic-update-slice_fusion.1, f32[384]{0:T(512)} %get-tuple-element.104, f32[384]{0:T(512)S(1)} %get-tuple-element.57, f32[384]{0:T(512)S(1)} %get-tuple-element.58, ...), kind=kLoop, calls=%fused_computation.289 | loop fusion | flops 57801728 | bytes 40187392 | tf_op jit(solution)/shard_map/reduce_sum | solution.py:87
  45.4 36.1 %all-gather.3.cloned.1.call-done = bf16[384,1536]{1,0:T(8,128)(2,1)} async-done(((bf16[24,1536]{1,0:T(8,128)(2,1)}), bf16[384,1536]{1,0:T(8,128)(2,1)}) %all-gather.3.cloned.1.call-update) | async-done | bytes 1179664 | tf_op jit(solution)/shard_map/all_gather | solution.py:83
  81.5 7.8 %multiply_convert_fusion = (bf16[1024,1536]{1,0:T(8,128)(2,1)}, f32[1024,1536]{1,0:T(8,128)}) fusion(f32[1536]{0:T(1024)} %param.19, bf16[1024,384]{1,0:T(8,128)(2,1)} %add_convert_fusion.1, bf16[384,1536]{1,0:T(8,128)(2,1)} %all-gather.3.cloned.1.call-done), kind=kOutput, calls=%fused_computation.58 | convolution fusion | flops 1223688192 | bytes 11409408 | tf_op jit(solution)/shard_map/dot_general | solution.py:92
  89.3 61.2 %all-gather.5.cloned.1.call-done = bf16[1536,384]{1,0:T(8,128)(2,1)} async-done(((bf16[96,384]{1,0:T(8,128)(2,1)}), bf16[1536,384]{1,0:T(8,128)(2,1)}) %all-gather.5.cloned.1.call-update) | async-done | bytes 1179664 | tf_op jit(solution)/shard_map/all_gather | solution.py:84
  150.5 4.2 fusion.105
  157.3 5.4 fusion.6
  162.7 2.0 fusion.107
  164.8 5.0 fusion.103
  169.7 3.0 fusion.67
  172.8 4.0 fusion.85
  178.2 5.2 fusion.116
  184.6 4.7 fusion.115
  190.1 3.5 collective-permute-start.5
  193.6 2.6 collective-permute-done.4
  197.2 1.3 collective-permute-start.6
  198.5 1.3 collective-permute-start.7
  201.0 3.3 collective-permute-done.7
  204.3 99.9 %all-reduce.4.cloned.1.call-done = f32[7,7,384]{2,1,0:T(8,128)} async-done(((f32[7,7,384]{2,1,0:T(8,128)}), f32[7,7,384]{2,1,0:T(8,128)}) %all-reduce.4.cloned.1.call-update) | async-done | bytes 75280 | tf_op jit(solution)/shard_map/psum | solution.py:150
  304.2 76.2 %reduce-scatter.5.cloned.1.call-done = f32[96,384]{1,0:T(8,128)} async-done(((f32[1536,384]{1,0:T(8,128)}), f32[96,384]{1,0:T(8,128)}) %reduce-scatter.5.cloned.1.call-update) | async-done | bytes 147472 | tf_op jit(solution)/shard_map/reduce_scatter | solution.py:153
  380.4 73.6 %reduce-scatter.3.cloned.1.call-done = f32[24,1536]{1,0:T(8,128)} async-done(((f32[384,1536]{1,0:T(8,128)}), f32[24,1536]{1,0:T(8,128)}) %reduce-scatter.3.cloned.1.call-update) | async-done | bytes 147472 | tf_op jit(solution)/shard_map/reduce_scatter | solution.py:152
  454.4 12.6 %broadcast_select_fusion = bf16[32,32,384]{2,1,0:T(8,128)(2,1)} fusion(pred[32]{0:T(512)(128)(4,1)} %copy-done.85, f32[384]{0:T(512)} %get-tuple-element.103, bf16[38,38,384]{2,1,0:T(8,128)(2,1)S(1)} %constant_dynamic-update-slice_fusion, f32[384]{0:T(512)} %get-tuple-element.104, f32[384]{0:T(512)S(1)} %copy-done.46, f32[384]{0:T(512)S(1)} %copy-done.48, ...), kind=kLoop, calls=%fused_computation.221 | loop fusion | flops 59375616 | bytes 40187424 | tf_op jit(solution)/shard_map/jit(_where)/select_n | solution.py:142
  467.0 130.2 %all-reduce.6.cloned.1.call-done = (f32[24,1536]{1,0:T(8,128)}, f32[96,384]{1,0:T(8,128)}, f32[7,7,384]{2,1,0:T(8,128)}) async-done(((f32[24,1536]{1,0:T(8,128)}, f32[96,384]{1,0:T(8,128)}, f32[7,7,384]{2,1,0:T(8,128)}), (f32[24,1536]{1,0:T(8,128)}, f32[96,384]{1,0:T(8,128)}, f32[7,7,384]{2,1,0:T(8,128)})) %all-reduce.6.cloned.1.call-update) | async-done | bytes 370192 | tf_op jit(solution)/shard_map/psum | solution.py:155
  597.3 1.6 broadcast_multiply_fusion.2
  598.8 1.5 broadcast_multiply_fusion.3
  600.4 1.6 broadcast_multiply_fusion.1
  (287 shorter events, 15.2 us)
Async XLA Ops:
  7.2 74.3 %all-gather.3.cloned.1.call-start = ((), (), s32[]{:S(2)}) async-start(), calls=%async_computation.2 | async-start | bytes 1253376 | tf_op jit(solution)/shard_map/all_gather | solution.py:83
  7.9 142.6 %all-gather.5.cloned.1.call-start = ((), (), s32[]{:S(2)}) async-start(), calls=%async_computation.3 | async-start | bytes 1253376 | tf_op jit(solution)/shard_map/all_gather | solution.py:84
  12.1 9.8 %collective-permute-start = (bf16[32,3,384]{2,1,0:T(4,128)(2,1)S(1)}, bf16[32,3,384]{2,1,0:T(4,128)(2,1)S(1)}, u32[]{:S(2)}, u32[]{:S(2)}) collective-permute-start(bf16[32,3,384]{2,1,0:T(4,128)(2,1)S(1)} %get-tuple-element.119), channel_id=1, source_target_pairs={{0,1},{1,2},{2,3},{3,4},{4,5},{5,6},{6,7},{7,8},{8,9},{9,10},{10,1... | collective-permute-start | bytes 221192 | tf_op jit(solution)/shard_map/ppermute | solution.py:20
  14.1 7.9 %collective-permute-start.1 = (bf16[32,3,384]{2,1,0:T(4,128)(2,1)S(1)}, bf16[32,3,384]{2,1,0:T(4,128)(2,1)S(1)}, u32[]{:S(2)}, u32[]{:S(2)}) collective-permute-start(bf16[32,3,384]{2,1,0:T(4,128)(2,1)S(1)} %get-tuple-element.120), channel_id=1, source_target_pairs={{1,0},{2,1},{3,2},{4,3},{5,4},{6,5},{7,6},{8,7},{9,8},{10,9},{11,1... | collective-permute-start | bytes 221192 | tf_op jit(solution)/shard_map/ppermute | solution.py:21
  18.0 286.2 %all-reduce.4.cloned.1.call-start = ((), (), s32[]{:S(2)}) async-start(), calls=%async_computation.6 | async-start | bytes 172032 | tf_op jit(solution)/shard_map/psum | solution.py:150
  22.6 3.4 collective-permute-start.2
  24.7 5.8 collective-permute-start.3
  178.2 202.3 %reduce-scatter.5.cloned.1.call-start = ((), (), s32[]{:S(2)}) async-start(), calls=%async_computation.5 | async-start | bytes 2506752 | tf_op jit(solution)/shard_map/reduce_scatter | solution.py:153
  183.4 270.6 %reduce-scatter.3.cloned.1.call-start = ((), (), s32[]{:S(2)}) async-start(), calls=%async_computation.4 | async-start | bytes 2506752 | tf_op jit(solution)/shard_map/reduce_scatter | solution.py:152
  189.3 408.0 %all-reduce.6.cloned.1.call-start = ((), (), s32[]{:S(2)}) async-start(), calls=%async_computation.7 | async-start | bytes 761856 | tf_op jit(solution)/shard_map/psum | solution.py:155
  189.4 6.8 %collective-permute-start.4 = (bf16[32,3,384]{2,1,0:T(4,128)(2,1)S(1)}, bf16[32,3,384]{2,1,0:T(4,128)(2,1)S(1)}, u32[]{:S(2)}, u32[]{:S(2)}) collective-permute-start(bf16[32,3,384]{2,1,0:T(4,128)(2,1)S(1)} %get-tuple-element.117), channel_id=1, source_target_pairs={{0,1},{1,2},{2,3},{3,4},{4,5},{5,6},{6,7},{7,8},{8,9},{9,10},{10,1... | collective-permute-start | bytes 221192 | tf_op jit(solution)/shard_map/ppermute | solution.py:20
  190.1 6.1 %collective-permute-start.5 = (bf16[32,3,384]{2,1,0:T(4,128)(2,1)S(1)}, bf16[32,3,384]{2,1,0:T(4,128)(2,1)S(1)}, u32[]{:S(2)}, u32[]{:S(2)}) collective-permute-start(bf16[32,3,384]{2,1,0:T(4,128)(2,1)S(1)} %get-tuple-element.118), channel_id=1, source_target_pairs={{1,0},{2,1},{3,2},{4,3},{5,4},{6,5},{7,6},{8,7},{9,8},{10,9},{11,1... | collective-permute-start | bytes 221192 | tf_op jit(solution)/shard_map/ppermute | solution.py:21
  196.8 257.2 %copy-start.1 = (bf16[32,32,384]{2,1,0:T(8,128)(2,1)S(1)}, bf16[32,32,384]{2,1,0:T(8,128)(2,1)}, u32[]{:S(2)}) copy-start(bf16[32,32,384]{2,1,0:T(8,128)(2,1)} %param.23) | copy-start | bytes 2359300
  196.8 257.2 %copy-start.8 = (f32[384]{0:T(512)S(1)}, f32[384]{0:T(512)}, u32[]{:S(2)}) copy-start(f32[384]{0:T(512)} %copy-done.7) | copy-start | bytes 4612
  196.8 257.2 %copy-start.10 = (f32[384]{0:T(512)S(1)}, f32[384]{0:T(512)}, u32[]{:S(2)}) copy-start(f32[384]{0:T(512)} %copy-done.9) | copy-start | bytes 4612
  196.8 257.2 %copy-start.12 = (f32[384]{0:T(512)S(1)}, f32[384]{0:T(512)}, u32[]{:S(2)}) copy-start(f32[384]{0:T(512)} %copy-done.11) | copy-start | bytes 4612
  196.9 257.2 %copy-start.14 = (f32[384]{0:T(512)S(1)}, f32[384]{0:T(512)}, u32[]{:S(2)}) copy-start(f32[384]{0:T(512)} %copy-done.13) | copy-start | bytes 4612
  196.9 257.2 %copy-start.16 = (f32[384]{0:T(512)S(1)}, f32[384]{0:T(512)}, u32[]{:S(2)}) copy-start(f32[384]{0:T(512)} %copy-done.15) | copy-start | bytes 4612
  196.9 257.2 %copy-start.18 = (f32[384]{0:T(512)S(1)}, f32[384]{0:T(512)}, u32[]{:S(2)}) copy-start(f32[384]{0:T(512)} %copy-done.17) | copy-start | bytes 4612
  196.9 257.2 %copy-start.20 = (f32[384]{0:T(512)S(1)}, f32[384]{0:T(512)}, u32[]{:S(2)}) copy-start(f32[384]{0:T(512)} %copy-done.19) | copy-start | bytes 4612
  196.9 257.2 %copy-start.22 = (f32[384]{0:T(512)S(1)}, f32[384]{0:T(512)}, u32[]{:S(2)}) copy-start(f32[384]{0:T(512)} %copy-done.21) | copy-start | bytes 4612
  196.9 257.2 %copy-start.24 = (f32[384]{0:T(512)S(1)}, f32[384]{0:T(512)}, u32[]{:S(2)}) copy-start(f32[384]{0:T(512)} %copy-done.23) | copy-start | bytes 4612
  196.9 257.2 %copy-start.26 = (f32[384]{0:T(512)S(1)}, f32[384]{0:T(512)}, u32[]{:S(2)}) copy-start(f32[384]{0:T(512)} %copy-done.25) | copy-start | bytes 4612
  196.9 257.2 %copy-start.28 = (f32[384]{0:T(512)S(1)}, f32[384]{0:T(512)}, u32[]{:S(2)}) copy-start(f32[384]{0:T(512)} %copy-done.27) | copy-start | bytes 4612
  196.9 257.2 %copy-start.30 = (f32[384]{0:T(512)S(1)}, f32[384]{0:T(512)}, u32[]{:S(2)}) copy-start(f32[384]{0:T(512)} %copy-done.29) | copy-start | bytes 4612
  196.9 257.2 %copy-start.32 = (f32[384]{0:T(512)S(1)}, f32[384]{0:T(512)}, u32[]{:S(2)}) copy-start(f32[384]{0:T(512)} %copy-done.31) | copy-start | bytes 4612
  197.0 257.2 %copy-start.34 = (f32[384]{0:T(512)S(1)}, f32[384]{0:T(512)}, u32[]{:S(2)}) copy-start(f32[384]{0:T(512)} %copy-done.33) | copy-start | bytes 4612
  197.0 257.2 %copy-start.36 = (f32[384]{0:T(512)S(1)}, f32[384]{0:T(512)}, u32[]{:S(2)}) copy-start(f32[384]{0:T(512)} %copy-done.35) | copy-start | bytes 4612
  197.0 257.2 %copy-start.38 = (f32[384]{0:T(512)S(1)}, f32[384]{0:T(512)}, u32[]{:S(2)}) copy-start(f32[384]{0:T(512)} %copy-done.37) | copy-start | bytes 4612
  197.0 257.2 %copy-start.40 = (f32[384]{0:T(512)S(1)}, f32[384]{0:T(512)}, u32[]{:S(2)}) copy-start(f32[384]{0:T(512)} %copy-done.39) | copy-start | bytes 4612
  197.2 2.6 collective-permute-start.6
  198.5 5.7 collective-permute-start.7
  (78 other events, 6207.3 us)
Sparse Core Ops, SparseCore 0:
  9.8 71.6 all-gather.2
  83.3 67.1 all-gather.4
  178.3 125.8 all-reduce.3
  306.8 73.6 reduce-scatter.4
  383.0 70.9 reduce-scatter.2
  456.9 140.2 all-reduce.5
